TPU v7x, 512 devices: a whole 4x4x16 slice. The times are simulated.
512 devices in a mesh: dp: 64 (over x, z_lo, core), seq: 8 (over y, z_hi).
Axes of the slice: x: 4, y: 4, z: 16 (z_hi: 2, z_lo: 8; z = z_hi * 8 + z_lo), core: 2. Of those that a mesh axis runs over, the one named last changes fastest.
Arguments:
- queries: bfloat16 [65536, 6144], P(('dp', 'seq')), may hold values from -8 to 8
- latent: bfloat16 [65536, 512], P(('dp', 'seq')), may hold values from -24 to 24
- key_rope: bfloat16 [65536, 64], P(('dp', 'seq')), may hold values from -8 to 8
- up_weight: bfloat16 [512, 8192], P(None, 'seq'), may hold values from -0.25 to 0.25
- out_grad: bfloat16 [65536, 4096], P(('dp', 'seq')), may hold values from -6 to 6
Outputs:
- latent_grad: float32 [65536, 512], P(('dp', 'seq'))
- weight_grad: float32 [512, 8192], P('dp', 'seq')
All inputs are finite; a program needn't handle non-finite values.
Results may differ from a plain program's by a relative error of at most 0.0065.
Values may be sent and summed in bfloat16 or wider, within the bound.
No kernel may reach another device: no remote copies, remote signals or barrier semaphores. Data moves between devices by JAX's collectives and lax.ppermute only.
A program may use at most 64 MiB of HBM per device.

v0:
```python
import math
import jax
import jax.numpy as jnp
from jax import lax
from jax.sharding import Mesh
from jax.sharding import PartitionSpec as P

NOPE = 128
ROPE = 64
VDIM = 128
SEQ = ("seq_0", "seq_1")
DP_SEQ = ("dp", "seq_0", "seq_1")


def in_one_piece(arrays, axis, dim, along):
    widths = [a.shape[along] for a in arrays]
    both = jnp.concatenate(arrays, axis=along)
    result = lax.all_gather(both, axis, axis=dim, tiled=True)
    return tuple(jnp.split(result, [sum(widths[:k]) for k in range(1, len(widths))], axis=along))


def scatter_axes(array, axes, dim):
    if not axes:
        return array
    nearer = lax.psum_scatter(array, axes[0], scatter_dimension=dim, tiled=True)
    return scatter_axes(nearer, axes[1:], dim)


def cut_along(array, dim, length):
    before, after = (array.shape[:dim], array.shape[dim + 1 :])
    return jnp.moveaxis(array.reshape(*before, length, -1, *after), dim, 0)


def sum_at_owner(array, axis, dim):
    pieces = cut_along(array, dim, lax.axis_size(axis))
    arrived = lax.all_to_all(pieces, axis, split_axis=0, concat_axis=0, tiled=True)
    return arrived.sum(axis=0)


def per_device(queries, latent, key_rope, up_weight, out_grad):
    query_width = NOPE + ROPE
    kv_width = NOPE + VDIM
    score_scale = query_width ** (-0.5)
    latent_full, rope_full = in_one_piece((latent, key_rope), SEQ, 0, 1)
    length = latent_full.shape[0]
    local_heads = up_weight.shape[1] // kv_width
    kv_cols = jnp.dot(latent_full, up_weight, preferred_element_type=jnp.float32).astype(
        jnp.bfloat16
    )
    block_rows = math.gcd(length, 512)

    def head_block(head_index, query_all, grad_out):
        kv_all = lax.dynamic_slice_in_dim(kv_cols, head_index * kv_width, kv_width, 1)
        query_nope = query_all[:, :NOPE]
        query_rope = query_all[:, NOPE:]
        keys_nope = kv_all[:, :NOPE]
        values = kv_all[:, NOPE:]
        key_grad = jnp.zeros((length, NOPE), jnp.float32)
        value_grad = jnp.zeros((length, VDIM), jnp.float32)
        for segment in range(length // block_rows):
            row_start = segment * block_rows
            row_end = row_start + block_rows
            scores = jnp.dot(
                query_nope[row_start:row_end],
                keys_nope[:row_end].T,
                preferred_element_type=jnp.float32,
            )
            scores = scores + jnp.dot(
                query_rope[row_start:row_end],
                rope_full[:row_end].T,
                preferred_element_type=jnp.float32,
            )
            scores = scores * score_scale
            query_pos = row_start + lax.broadcasted_iota(jnp.int32, (block_rows, row_end), 0)
            key_pos = lax.broadcasted_iota(jnp.int32, (block_rows, row_end), 1)
            scores = jnp.where(key_pos <= query_pos, scores, jnp.float32(-1e30))
            row_max = jnp.max(scores, axis=1, keepdims=True)
            expo = jnp.exp(scores - row_max)
            attend = expo / jnp.sum(expo, axis=1, keepdims=True)
            attend_rounded = attend.astype(jnp.bfloat16)
            grad_rows = grad_out[row_start:row_end]
            value_grad = value_grad.at[:row_end].add(
                jnp.dot(attend_rounded.T, grad_rows, preferred_element_type=jnp.float32)
            )
            prob_grad = jnp.dot(grad_rows, values[:row_end].T, preferred_element_type=jnp.float32)
            row_dot = jnp.sum(attend * prob_grad, axis=1, keepdims=True)
            score_grad = (attend * (prob_grad - row_dot) * score_scale).astype(jnp.bfloat16)
            key_grad = key_grad.at[:row_end].add(
                jnp.dot(
                    score_grad.T, query_nope[row_start:row_end], preferred_element_type=jnp.float32
                )
            )
        return jnp.concatenate([key_grad, value_grad], axis=1).astype(jnp.bfloat16)

    start_cols = jnp.zeros((length, local_heads * kv_width), jnp.bfloat16)
    query_heads, grad_heads = (
        lax.all_to_all(queries, SEQ, split_axis=1, concat_axis=0, tiled=True),
        lax.all_to_all(out_grad, SEQ, split_axis=1, concat_axis=0, tiled=True),
    )

    def one_head(head_index, grad_cols):
        query_all = lax.dynamic_slice_in_dim(query_heads, head_index * query_width, query_width, 1)
        grad_out = lax.dynamic_slice_in_dim(grad_heads, head_index * VDIM, VDIM, 1)
        joined = head_block(head_index, query_all, grad_out)
        return lax.dynamic_update_slice_in_dim(grad_cols, joined, head_index * kv_width, 1)

    grad_cols = lax.fori_loop(0, local_heads, one_head, start_cols)
    latent_part = jnp.dot(grad_cols, up_weight.T, preferred_element_type=jnp.float32)
    latent_grad = scatter_axes(latent_part, SEQ, 0)
    replicas = lax.axis_size("dp")
    weight_full = jnp.dot(latent_full.T, grad_cols, preferred_element_type=jnp.float32)
    summed = sum_at_owner(weight_full, "dp", 0)
    return (latent_grad, summed / replicas)


def solution(mesh):
    torus = Mesh(mesh.devices.reshape(mesh.shape["dp"], 4, 2), ("dp", "seq_0", "seq_1"))
    in_specs = (P(DP_SEQ, None), P(DP_SEQ, None), P(DP_SEQ, None), P(None, SEQ), P(DP_SEQ, None))
    out_specs = (P(DP_SEQ, None), P("dp", SEQ))
    return jax.shard_map(
        per_device, mesh=torus, in_specs=in_specs, out_specs=out_specs, check_vma=False
    )
```

profile of v0, /device:TPU:1, one launch (start us, length us, event | category | flops | bytes accessed | tf_op | source)
XLA Modules:
  0.0 438.4 jit_solution(139880134441688414)
XLA Ops:
  7.2 2.5 copy.15
  9.6 18.3 %all-to-all-start.1 = ((bf16[128,8,512]{2,0,1:T(8,128)(2,1)}), bf16[128,8,512]{2,0,1:T(8,128)(2,1)}, u32[]{:S(2)}, u32[]{:S(2)}) async-start(bf16[128,8,512]{2,0,1:T(8,128)(2,1)} %bitcast.20), calls=%async_computation.1 | async-start | bytes 2097152 | tf_op jit(solution)/shard_map/all_to_all | solution.py:98
  27.9 1.3 copy.14
  29.2 27.5 %all-to-all-done.1 = bf16[128,8,512]{2,0,1:T(8,128)(2,1)} async-done(((bf16[128,8,512]{2,0,1:T(8,128)(2,1)}), bf16[128,8,512]{2,0,1:T(8,128)(2,1)}, u32[]{:S(2)}, u32[]{:S(2)}) %all-to-all-start.1) | async-done | bytes 1048608 | tf_op jit(solution)/shard_map/all_to_all | solution.py:98
  56.7 3.6 all-to-all-start
  60.5 0.7 pad_maximum_fusion
  61.2 166.4 %all-gather.2.cloned.1.call-done = bf16[1024,576]{1,0:T(8,128)(2,1)} async-done(((bf16[128,576]{1,0:T(8,128)(2,1)}), bf16[1024,576]{1,0:T(8,128)(2,1)}) %all-gather.2.cloned.1.call-update) | async-done | bytes 1179664 | tf_op jit(solution)/shard_map/all_gather | solution.py:18
  227.6 3.8 convolution_convert_fusion
  231.4 1.6 broadcast_in_dim.43
  233.3 66.3 %while.35 = (s32[]{:T(128)}, bf16[1024,1024]{0,1:T(8,128)(2,1)}, bf16[1024,768]{1,0:T(8,128)(2,1)}, bf16[1024,1024]{1,0:T(8,128)(2,1)}, bf16[1024,64]{1,0:T(8,12...) while((s32[]{:T(128)}, bf16[1024,1024]{0,1:T(8,128)(2,1)}, ...), condition=%wide.region_7.8_spmd, body=%wide.region_0.7_spmd.sunk | while | flops 923268608 | bytes 33341852 | solution.py:107
  233.3 1.5 fusion.90
  234.8 1.3 fusion.91
  236.3 1.3 fusion.93
  237.5 1.3 multiply_reduce_fusion.5
  238.8 1.4 fusion.98
  240.3 1.5 fusion.94
  241.8 1.7 fusion.95
  243.5 0.5 fusion.96
  244.0 1.5 fusion.97
  245.5 1.7 multiply_reduce_fusion.4
  247.2 1.9 fusion.99
  249.1 0.9 maximum_dynamic-update-slice_fusion.2
  250.0 1.4 fusion.90
  251.3 1.3 fusion.91
  252.8 1.3 fusion.93
  254.1 1.3 multiply_reduce_fusion.5
  255.4 1.4 fusion.98
  256.8 1.5 fusion.94
  258.4 1.7 fusion.95
  260.0 0.5 fusion.96
  260.5 1.5 fusion.97
  262.1 1.7 multiply_reduce_fusion.4
  263.8 1.9 fusion.99
  265.7 0.9 maximum_dynamic-update-slice_fusion.2
  266.5 1.4 fusion.90
  267.9 1.3 fusion.91
  269.4 1.3 fusion.93
  270.7 1.3 multiply_reduce_fusion.5
  272.0 1.4 fusion.98
  273.4 1.5 fusion.94
  274.9 1.7 fusion.95
  276.6 0.5 fusion.96
  277.1 1.5 fusion.97
  278.6 1.7 multiply_reduce_fusion.4
  280.3 1.9 fusion.99
  282.2 0.9 maximum_dynamic-update-slice_fusion.2
  283.1 1.4 fusion.90
  284.4 1.3 fusion.91
  285.9 1.3 fusion.93
  287.2 1.3 multiply_reduce_fusion.5
  288.5 1.4 fusion.98
  289.9 1.5 fusion.94
  291.5 1.7 fusion.95
  293.1 0.5 fusion.96
  293.6 1.5 fusion.97
  295.2 1.7 multiply_reduce_fusion.4
  296.9 1.9 fusion.99
  298.8 0.8 maximum_dynamic-update-slice_fusion.2
  299.6 4.2 convolution_bitcast_fusion
  303.9 8.8 %all-to-all-start.2 = ((f32[64,8,1024]{2,1,0:T(8,128)}), f32[64,8,1024]{2,1,0:T(8,128)S(1)}, u32[]{:S(2)}, u32[]{:S(2)}) async-start(f32[64,8,1024]{2,1,0:T(8,128)} %convolution_bitcast_fusion), calls=%async_computation.4 | async-start | bytes 4194304 | tf_op jit(solution)/shard_map/all_to_all | solution.py:36
  312.7 4.3 fusion.52
  317.0 35.5 %reduce-scatter.3.cloned.1.call-done = f32[256,512]{1,0:T(8,128)} async-done(((f32[1024,512]{1,0:T(8,128)}), f32[256,512]{1,0:T(8,128)}) %reduce-scatter.3.cloned.1.call-update) | async-done | bytes 524304 | tf_op jit(solution)/shard_map/reduce_scatter | solution.py:25
  352.5 78.5 %all-to-all-done.2 = f32[64,8,1024]{2,1,0:T(8,128)S(1)} async-done(((f32[64,8,1024]{2,1,0:T(8,128)}), f32[64,8,1024]{2,1,0:T(8,128)S(1)}, u32[]{:S(2)}, u32[]{:S(2)}) %all-to-all-start.2) | async-done | bytes 2097184 | tf_op jit(solution)/shard_map/all_to_all | solution.py:36
  431.2 0.6 broadcast_multiply_fusion
  (32 shorter events, 1.5 us)
Async XLA Ops:
  7.2 220.4 %copy-start = (bf16[512,1024]{1,0:T(8,128)(2,1)S(1)}, bf16[512,1024]{1,0:T(8,128)(2,1)}, u32[]{:S(2)}) copy-start(bf16[512,1024]{1,0:T(8,128)(2,1)} %param.22) | copy-start | bytes 3145732
  7.2 20.7 %copy-start.3 = (bf16[128,6144]{1,0:T(8,128)(2,1)S(1)}, bf16[128,6144]{1,0:T(8,128)(2,1)}, u32[]{:S(2)}) copy-start(bf16[128,6144]{1,0:T(8,128)(2,1)} %param.19) | copy-start | bytes 4718596
  9.6 47.1 %all-to-all-start.1 = ((bf16[128,8,512]{2,0,1:T(8,128)(2,1)}), bf16[128,8,512]{2,0,1:T(8,128)(2,1)}, u32[]{:S(2)}, u32[]{:S(2)}) async-start(bf16[128,8,512]{2,0,1:T(8,128)(2,1)} %bitcast.20), calls=%async_computation.1 | async-start | bytes 2097152 | tf_op jit(solution)/shard_map/all_to_all | solution.py:98
  29.2 31.2 %copy-start.5 = (bf16[128,64]{0,1:T(8,128)(2,1)S(1)}, bf16[128,64]{0,1:T(8,128)(2,1)}, u32[]{:S(2)}) copy-start(bf16[128,64]{0,1:T(8,128)(2,1)} %param.21) | copy-start | bytes 49156
  29.2 31.3 %copy-start.4 = (bf16[128,512]{1,0:T(8,128)(2,1)S(1)}, bf16[128,512]{1,0:T(8,128)(2,1)}, u32[]{:S(2)}) copy-start(bf16[128,512]{1,0:T(8,128)(2,1)} %param.20) | copy-start | bytes 393220
  56.7 174.7 %all-to-all-start = ((bf16[128,8,768]{2,0,1:T(8,128)(2,1)}), bf16[128,8,768]{2,0,1:T(8,128)(2,1)S(1)}, u32[]{:S(2)}, u32[]{:S(2)}) async-start(bf16[128,8,768]{2,0,1:T(8,128)(2,1)} %bitcast.24), calls=%async_computation | async-start | bytes 3145728 | tf_op jit(solution)/shard_map/all_to_all | solution.py:97
  60.3 167.3 %all-gather.2.cloned.1.call-start = ((), (), s32[]{:S(2)}) async-start(), calls=%async_computation.5 | async-start | bytes 1474560 | tf_op jit(solution)/shard_map/all_gather | solution.py:18
  231.4 1.8 slice-start
  231.4 1.8 copy-start.2
  233.3 66.3 %copy-start.1 = (bf16[1024,576]{1,0:T(8,128)(2,1)S(1)}, bf16[1024,576]{1,0:T(8,128)(2,1)}, u32[]{:S(2)}) copy-start(bf16[1024,576]{1,0:T(8,128)(2,1)} %all-gather.2.cloned.1.call-done) | copy-start | bytes 3538948
  303.9 127.2 %all-to-all-start.2 = ((f32[64,8,1024]{2,1,0:T(8,128)}), f32[64,8,1024]{2,1,0:T(8,128)S(1)}, u32[]{:S(2)}, u32[]{:S(2)}) async-start(f32[64,8,1024]{2,1,0:T(8,128)} %convolution_bitcast_fusion), calls=%async_computation.4 | async-start | bytes 4194304 | tf_op jit(solution)/shard_map/all_to_all | solution.py:36
  312.6 39.9 %reduce-scatter.3.cloned.1.call-start = ((), (), s32[]{:S(2)}) async-start(), calls=%async_computation.6 | async-start | bytes 2621440 | tf_op jit(solution)/shard_map/reduce_scatter | solution.py:25
  317.0 114.9 %reduce-scatter.5.cloned.1.call-start = ((), (), s32[]{:S(2)}) async-start(), calls=%async_computation.7 | async-start | bytes 786432 | tf_op jit(solution)/shard_map/reduce_scatter | solution.py:25
Sparse Core Ops, SparseCore 0:
  64.9 162.6 all-gather.1
  317.1 35.3 reduce-scatter.2
  356.1 39.9 reduce-scatter.4
where the time goes:
time: 440 us; the launch traced here: 438 us
  waiting for transfers between devices  308 us (70%)
  matrix products  72.2 us (16%)
  starting transfers between devices  30.7 us (7%)
  between operations  13.8 us (3%)
  other arithmetic  7.73 us (2%)
  local copies, waits for them, and re-layouts  5.69 us (1%)
    all_gather x1, waiting for transfers between devices, in_one_piece(): result = lax.all_gather(both, axis, axis=dim, tiled=True)  166 us
    all_to_all x1, waiting for transfers between devices, sum_at_owner(): lax.all_to_all(pieces, axis, split_axis=0, concat_axis=0, tiled=True)  78.5 us
    reduce_scatter x2, waiting for transfers between devices, scatter_axes(): nearer = lax.psum_scatter(array, axes[0], scatter_dimension=dim, tiled=True)  35.5 us
    all_to_all x1, waiting for transfers between devices, per_device(): lax.all_to_all(out_grad, SEQ, split_axis=1, concat_axis=0, tiled=True)  27.5 us
    all_to_all x1, starting transfers between devices, per_device(): lax.all_to_all(out_grad, SEQ, split_axis=1, concat_axis=0, tiled=True)  18.3 us
    dot_general x8, matrix products, head_block(): jnp.dot(score_grad.T, query_nope[row_start:row_end], preferred_element_ty...  13.3 us
    dot_general x8, matrix products, head_block(): jnp.dot(grad_rows, values[:row_end].T, preferred_element_type=jnp.float32)  11.9 us
    dot_general x8, matrix products, head_block(): jnp.dot(query_rope[row_start:row_end], rope_full[:row_end].T, preferred_e...  11.9 us
  transfers between devices with their start and end apart: 6, of which 4 were waited for; matrix products, arithmetic and copies ran while one was open for 2% of the time, Pallas kernels for 0%

commit v1 on v0

--- a/solution.py
+++ b/solution.py
@@ -95,7 +95,10 @@
     start_cols = jnp.zeros((length, local_heads * kv_width), jnp.bfloat16)
     query_heads, grad_heads = (
         lax.all_to_all(queries, SEQ, split_axis=1, concat_axis=0, tiled=True),
-        lax.all_to_all(out_grad, SEQ, split_axis=1, concat_axis=0, tiled=True),
+        jnp.concatenate(
+            lax.all_to_all(jnp.stack(jnp.split(out_grad, lax.axis_size(SEQ), axis=1)), SEQ, 0, 0),
+            axis=0,
+        ),
     )
 
     def one_head(head_index, grad_cols):

time: 440 us -> 450 us (1.023)
  local copies, waits for them, and re-layouts: 5.69 us -> 15.9 us
    unnamed x13 -> x20, local copies, waits for them, and re-layouts: 0.4 us -> 11.4 us
where the time goes in v1:
time: 450 us; the launch traced here: 449 us
  waiting for transfers between devices  308 us (68%)
  matrix products  72.2 us (16%)
  starting transfers between devices  30.7 us (7%)
  local copies, waits for them, and re-layouts  15.9 us (4%)
  between operations  13.8 us (3%)
  other arithmetic  7.73 us (2%)
    all_gather x1, waiting for transfers between devices, in_one_piece(): result = lax.all_gather(both, axis, axis=dim, tiled=True)  166 us
    all_to_all x1, waiting for transfers between devices, sum_at_owner(): lax.all_to_all(pieces, axis, split_axis=0, concat_axis=0, tiled=True)  78.5 us
    reduce_scatter x2, waiting for transfers between devices, scatter_axes(): nearer = lax.psum_scatter(array, axes[0], scatter_dimension=dim, tiled=True)  35.5 us
    all_to_all x1, waiting for transfers between devices, per_device(): lax.all_to_all(jnp.stack(jnp.split(out_grad, lax.axis_size(SEQ), axis=1))...  27.5 us
    all_to_all x1, starting transfers between devices, per_device(): lax.all_to_all(jnp.stack(jnp.split(out_grad, lax.axis_size(SEQ), axis=1))...  18.3 us
    dot_general x8, matrix products, head_block(): jnp.dot(score_grad.T, query_nope[row_start:row_end], preferred_element_ty...  13.3 us
    dot_general x8, matrix products, head_block(): jnp.dot(grad_rows, values[:row_end].T, preferred_element_type=jnp.float32)  11.9 us
    dot_general x8, matrix products, head_block(): jnp.dot(query_rope[row_start:row_end], rope_full[:row_end].T, preferred_e...  11.9 us
  transfers between devices with their start and end apart: 6, of which 4 were waited for; matrix products, arithmetic and copies ran while one was open for 2% of the time, Pallas kernels for 0%

profile of v1, /device:TPU:1, one launch (start us, length us, event | category | flops | bytes accessed | tf_op | source)
XLA Modules:
  0.0 448.5 jit_solution(4932824407736646376)
XLA Ops:
  7.2 1.7 bitcast_dynamic-update-slice_fusion.7
  8.9 1.6 bitcast_dynamic-update-slice_fusion.6
  10.4 1.6 bitcast_dynamic-update-slice_fusion.5
  12.0 1.6 bitcast_dynamic-update-slice_fusion.4
  13.6 1.6 bitcast_dynamic-update-slice_fusion.3
  15.1 1.6 bitcast_dynamic-update-slice_fusion.2
  16.7 1.6 bitcast_dynamic-update-slice_fusion.1
  18.2 1.6 bitcast_dynamic-update-slice_fusion
  19.8 18.3 %all-to-all-start.1 = ((bf16[8,128,512]{2,1,0:T(8,128)(2,1)}), bf16[8,128,512]{2,1,0:T(8,128)(2,1)}, u32[]{:S(2)}, u32[]{:S(2)}) async-start(bf16[8,128,512]{2,1,0:T(8,128)(2,1)} %bitcast_dynamic-update-slice_fusion), calls=%async_computation.1 | async-start | bytes 2097152 | tf_op jit(solution)/shard_map/all_to_all | solution.py:99
  38.1 1.3 copy.11
  39.4 27.5 %all-to-all-done.1 = bf16[8,128,512]{2,1,0:T(8,128)(2,1)} async-done(((bf16[8,128,512]{2,1,0:T(8,128)(2,1)}), bf16[8,128,512]{2,1,0:T(8,128)(2,1)}, u32[]{:S(2)}, u32[]{:S(2)}) %all-to-all-start.1) | async-done | bytes 1048608 | tf_op jit(solution)/shard_map/all_to_all | solution.py:99
  66.9 3.6 all-to-all-start
  71.4 166.4 %all-gather.2.cloned.1.call-done = bf16[1024,576]{1,0:T(8,128)(2,1)} async-done(((bf16[128,576]{1,0:T(8,128)(2,1)}), bf16[1024,576]{1,0:T(8,128)(2,1)}) %all-gather.2.cloned.1.call-update) | async-done | bytes 1179664 | tf_op jit(solution)/shard_map/all_gather | solution.py:18
  237.8 3.8 convolution_convert_fusion
  241.6 1.6 broadcast_in_dim.43
  243.5 66.3 %while.35 = (s32[]{:T(128)}, bf16[1024,1024]{0,1:T(8,128)(2,1)}, bf16[1024,768]{1,0:T(8,128)(2,1)}, bf16[1024,1024]{1,0:T(8,128)(2,1)}, bf16[1024,64]{1,0:T(8,12...) while((s32[]{:T(128)}, bf16[1024,1024]{0,1:T(8,128)(2,1)}, ...), condition=%wide.region_7.8_spmd, body=%wide.region_0.7_spmd.sunk | while | flops 923268608 | bytes 33341852 | solution.py:110
  243.5 1.5 fusion.90
  244.9 1.3 fusion.91
  246.4 1.3 fusion.93
  247.7 1.3 multiply_reduce_fusion.5
  249.0 1.4 fusion.98
  250.4 1.5 fusion.94
  252.0 1.7 fusion.95
  254.1 1.5 fusion.97
  255.7 1.7 multiply_reduce_fusion.4
  257.4 1.9 fusion.99
  259.3 0.9 maximum_dynamic-update-slice_fusion.2
  260.1 1.4 fusion.90
  261.5 1.3 fusion.91
  263.0 1.3 fusion.93
  264.3 1.3 multiply_reduce_fusion.5
  265.6 1.4 fusion.98
  267.0 1.5 fusion.94
  268.5 1.7 fusion.95
  270.7 1.5 fusion.97
  272.2 1.7 multiply_reduce_fusion.4
  273.9 1.9 fusion.99
  275.8 0.9 maximum_dynamic-update-slice_fusion.2
  276.7 1.4 fusion.90
  278.1 1.3 fusion.91
  279.6 1.3 fusion.93
  280.8 1.3 multiply_reduce_fusion.5
  282.1 1.4 fusion.98
  283.6 1.5 fusion.94
  285.1 1.7 fusion.95
  287.3 1.5 fusion.97
  288.8 1.7 multiply_reduce_fusion.4
  290.5 1.9 fusion.99
  292.4 0.9 maximum_dynamic-update-slice_fusion.2
  293.2 1.4 fusion.90
  294.6 1.3 fusion.91
  296.1 1.3 fusion.93
  297.4 1.3 multiply_reduce_fusion.5
  298.7 1.4 fusion.98
  300.1 1.5 fusion.94
  301.6 1.7 fusion.95
  303.8 1.5 fusion.97
  305.3 1.7 multiply_reduce_fusion.4
  307.0 1.9 fusion.99
  309.8 4.2 convolution_bitcast_fusion
  314.0 8.8 %all-to-all-start.2 = ((f32[64,8,1024]{2,1,0:T(8,128)}), f32[64,8,1024]{2,1,0:T(8,128)S(1)}, u32[]{:S(2)}, u32[]{:S(2)}) async-start(f32[64,8,1024]{2,1,0:T(8,128)} %convolution_bitcast_fusion), calls=%async_computation.4 | async-start | bytes 4194304 | tf_op jit(solution)/shard_map/all_to_all | solution.py:36
  322.8 4.3 fusion.52
  327.2 35.5 %reduce-scatter.3.cloned.1.call-done = f32[256,512]{1,0:T(8,128)} async-done(((f32[1024,512]{1,0:T(8,128)}), f32[256,512]{1,0:T(8,128)}) %reduce-scatter.3.cloned.1.call-update) | async-done | bytes 524304 | tf_op jit(solution)/shard_map/reduce_scatter | solution.py:25
  362.7 78.5 %all-to-all-done.2 = f32[64,8,1024]{2,1,0:T(8,128)S(1)} async-done(((f32[64,8,1024]{2,1,0:T(8,128)}), f32[64,8,1024]{2,1,0:T(8,128)S(1)}, u32[]{:S(2)}, u32[]{:S(2)}) %all-to-all-start.2) | async-done | bytes 2097184 | tf_op jit(solution)/shard_map/all_to_all | solution.py:36
  (39 shorter events, 5.7 us)
Async XLA Ops:
  7.2 230.6 %copy-start = (bf16[512,1024]{1,0:T(8,128)(2,1)S(1)}, bf16[512,1024]{1,0:T(8,128)(2,1)}, u32[]{:S(2)}) copy-start(bf16[512,1024]{1,0:T(8,128)(2,1)} %param.22) | copy-start | bytes 3145732
  7.2 30.9 %copy-start.3 = (bf16[128,6144]{1,0:T(8,128)(2,1)S(1)}, bf16[128,6144]{1,0:T(8,128)(2,1)}, u32[]{:S(2)}) copy-start(bf16[128,6144]{1,0:T(8,128)(2,1)} %param.19) | copy-start | bytes 4718596
  19.8 47.1 %all-to-all-start.1 = ((bf16[8,128,512]{2,1,0:T(8,128)(2,1)}), bf16[8,128,512]{2,1,0:T(8,128)(2,1)}, u32[]{:S(2)}, u32[]{:S(2)}) async-start(bf16[8,128,512]{2,1,0:T(8,128)(2,1)} %bitcast_dynamic-update-slice_fusion), calls=%async_computation.1 | async-start | bytes 2097152 | tf_op jit(solution)/shard_map/all_to_all | solution.py:99
  39.3 31.2 %copy-start.5 = (bf16[128,64]{0,1:T(8,128)(2,1)S(1)}, bf16[128,64]{0,1:T(8,128)(2,1)}, u32[]{:S(2)}) copy-start(bf16[128,64]{0,1:T(8,128)(2,1)} %param.21) | copy-start | bytes 49156
  39.3 31.3 %copy-start.4 = (bf16[128,512]{1,0:T(8,128)(2,1)S(1)}, bf16[128,512]{1,0:T(8,128)(2,1)}, u32[]{:S(2)}) copy-start(bf16[128,512]{1,0:T(8,128)(2,1)} %param.20) | copy-start | bytes 393220
  66.9 174.7 %all-to-all-start = ((bf16[128,8,768]{2,0,1:T(8,128)(2,1)}), bf16[128,8,768]{2,0,1:T(8,128)(2,1)S(1)}, u32[]{:S(2)}, u32[]{:S(2)}) async-start(bf16[128,8,768]{2,0,1:T(8,128)(2,1)} %bitcast.34), calls=%async_computation | async-start | bytes 3145728 | tf_op jit(solution)/shard_map/all_to_all | solution.py:97
  70.5 167.3 %all-gather.2.cloned.1.call-start = ((), (), s32[]{:S(2)}) async-start(), calls=%async_computation.5 | async-start | bytes 1474560 | tf_op jit(solution)/shard_map/all_gather | solution.py:18
  241.6 1.8 slice-start
  241.6 1.8 copy-start.2
  243.4 66.3 %copy-start.1 = (bf16[1024,576]{1,0:T(8,128)(2,1)S(1)}, bf16[1024,576]{1,0:T(8,128)(2,1)}, u32[]{:S(2)}) copy-start(bf16[1024,576]{1,0:T(8,128)(2,1)} %all-gather.2.cloned.1.call-done) | copy-start | bytes 3538948
  314.0 127.2 %all-to-all-start.2 = ((f32[64,8,1024]{2,1,0:T(8,128)}), f32[64,8,1024]{2,1,0:T(8,128)S(1)}, u32[]{:S(2)}, u32[]{:S(2)}) async-start(f32[64,8,1024]{2,1,0:T(8,128)} %convolution_bitcast_fusion), calls=%async_computation.4 | async-start | bytes 4194304 | tf_op jit(solution)/shard_map/all_to_all | solution.py:36
  322.8 39.9 %reduce-scatter.3.cloned.1.call-start = ((), (), s32[]{:S(2)}) async-start(), calls=%async_computation.6 | async-start | bytes 2621440 | tf_op jit(solution)/shard_map/reduce_scatter | solution.py:25
  327.1 114.9 %reduce-scatter.5.cloned.1.call-start = ((), (), s32[]{:S(2)}) async-start(), calls=%async_computation.7 | async-start | bytes 786432 | tf_op jit(solution)/shard_map/reduce_scatter | solution.py:25
Sparse Core Ops, SparseCore 0:
  75.1 162.6 all-gather.1
  327.2 35.3 reduce-scatter.2
  366.3 39.9 reduce-scatter.4
